TPU v7x, 32 devices: a whole 2x2x4 slice. The times are simulated.
32 devices in a mesh: inp: 8 (over y, x, core), tim: 4 (over z).
Axes of the slice: x: 2, y: 2, z: 4, core: 2. Of those that a mesh axis runs over, the one named last changes fastest.
Arguments:
- voltages: bfloat16 [2, 1024, 8192], P(None, 'inp', 'tim'), may hold values from -6 to 6
- fir_taps: int32 [4, 512], replicated, may hold values from -2048 to 2047
- station_flags: int32 [512, 4], P('inp', 'tim'), may hold values 0 or 1
- tile_pairs: int32 [528, 2], replicated, may hold values from 0 to 31, as said below
Outputs:
- visibilities: float32 [512, 528, 2, 1024], P(('inp', 'tim'))
Inputs may be any that keep to these rules, and one draw needn't show every extreme that they name: `tile_pairs`: each row holds tile indices I <= J, every such pair of the 32 blocks appears exactly once, in an order drawn from the seed.
All inputs are finite; a program needn't handle non-finite values. No bound on the sum of `station_flags` on one device may be relied on, other than what follows from the above.
Results may differ from a plain program's by a relative error of at most 0.004.
Values may be sent and summed in bfloat16 or wider, within the bound.
No kernel may reach another device: no remote copies, remote signals or barrier semaphores. Data moves between devices by JAX's collectives and lax.ppermute only.
A program may use at most 256 MiB of HBM per device.

v0:
```python
import math

import jax
import jax.numpy as jnp
from jax import lax
from jax.sharding import PartitionSpec as P

TB = 32
FLAGRUN = 4


def shifted(block, axis, distance):
    devices = range(lax.axis_size(axis))
    route = [(i - distance, i) for i in devices if i - distance in devices]
    return lax.ppermute(block, axis, route)


def body(voltages, fir_taps, station_flags, tile_pairs):
    width = voltages.shape[1]
    taps_count = fir_taps.shape[0]
    chans = fir_taps.shape[1]
    local_spectra = voltages.shape[2] // chans
    frames = voltages.reshape(2, width, local_spectra, chans)
    tail = frames[:, :, local_spectra - (taps_count - 1) :, :]
    earlier = shifted(tail, "tim", 1)
    extended = jnp.concatenate([earlier, frames], axis=2).astype(jnp.float32)
    coeffs = fir_taps.astype(jnp.float32) * (1.0 / (2048.0 * math.sqrt(taps_count * chans)))
    filtered = jnp.zeros((2, width, local_spectra, chans), jnp.float32)
    for offset in range(taps_count):
        begin = taps_count - 1 - offset
        filtered = filtered + coeffs[offset] * extended[:, :, begin : begin + local_spectra, :]
    first_rows = filtered[0].reshape(width * local_spectra, chans)
    second_rows = filtered[1].reshape(width * local_spectra, chans)
    positions = jnp.arange(chans, dtype=jnp.int32)
    phase = positions[:, None] * positions[None, :] % chans
    angle = phase.astype(jnp.float32) * (2.0 * math.pi / chans)
    cosine = jnp.cos(angle)
    sine = jnp.sin(angle)
    highest = lax.Precision.HIGHEST
    real_out = jnp.dot(
        first_rows, cosine, precision=highest, preferred_element_type=jnp.float32
    ) + jnp.dot(second_rows, sine, precision=highest, preferred_element_type=jnp.float32)
    imag_out = jnp.dot(
        second_rows, cosine, precision=highest, preferred_element_type=jnp.float32
    ) - jnp.dot(first_rows, sine, precision=highest, preferred_element_type=jnp.float32)
    transformed = jnp.concatenate([real_out, imag_out], axis=-1)
    flag_full = jnp.repeat(jnp.repeat(station_flags, 2, axis=0), FLAGRUN, axis=1).astype(
        jnp.bfloat16
    )
    spectra = transformed.astype(jnp.bfloat16) * flag_full.reshape(width * local_spectra, 1)
    n_inputs = lax.axis_size("inp")
    n_times = lax.axis_size("tim")
    per_device = chans // (n_inputs * n_times)
    total_inputs = width * n_inputs
    total_spectra = local_spectra * n_times
    sectioned = spectra.reshape(width, local_spectra, 2, n_inputs, n_times, per_device)
    owned = lax.all_to_all(
        lax.all_to_all(sectioned, "tim", split_axis=4, concat_axis=1, tiled=True),
        "inp",
        split_axis=3,
        concat_axis=0,
        tiled=True,
    )
    owned = owned.reshape(total_inputs, total_spectra, 2, per_device)
    ordered = jnp.transpose(owned, (3, 2, 0, 1))
    blocks = total_inputs // TB
    scale = 1.0 / total_spectra
    first_index = tile_pairs[:, 0]
    second_index = tile_pairs[:, 1]

    def one_channel(plane):
        real_rows = plane[0].reshape(blocks, TB, total_spectra)
        imag_rows = plane[1].reshape(blocks, TB, total_spectra)
        right_side = jnp.concatenate([real_rows, imag_rows], axis=2)
        turned = jnp.concatenate([imag_rows, -real_rows], axis=2)
        real_grid = jnp.einsum(
            "iuk,jvk->ijuv", right_side, right_side, preferred_element_type=jnp.float32
        )
        imag_grid = jnp.einsum(
            "iuk,jvk->ijuv", turned, right_side, preferred_element_type=jnp.float32
        )
        grid = jnp.stack([real_grid, imag_grid], axis=2) * scale
        picked = grid[first_index, second_index]
        return picked.reshape(picked.shape[0], 2, TB * TB)

    return lax.map(one_channel, ordered)


def solution(mesh):
    in_specs = (P(None, "inp", "tim"), P(), P("inp", "tim"), P())
    out_specs = P(("inp", "tim"), None, None, None)
    return jax.shard_map(body, mesh=mesh, in_specs=in_specs, out_specs=out_specs, check_vma=False)
```

profile of v0, /device:TPU:0, one launch (start us, length us, event | category | flops | bytes accessed | tf_op | source)
XLA Modules:
  0.0 1440.6 jit_solution(14668888947590495330)
XLA Ops:
  8.6 15.1 %collective-permute-done = bf16[2,128,3,512]{3,1,2,0:T(8,128)(2,1)S(1)} collective-permute-done((bf16[2,128,3,512]{3,1,2,0:T(8,128)(2,1)S(1)}, bf16[2,128,3,512]{3,1,2,0:T(8,128)(2,1)S(1)}, u32[]{:S(2)}, u32[]{:S(2)}) %collective-permute-start) | collective-permute-done | bytes 786464 | tf_op jit(solution)/shard_map/ppermute | solution.py:15
  54.2 8.1 convert_element_type.38
  62.3 8.5 broadcast_multiply_fusion
  70.7 12.4 copy.29
  83.1 30.4 %all_to_all.33 = bf16[128,4,2,8,4,16]{0,5,3,2,1,4:T(8,128)(2,1)S(1)} all-to-all(bf16[128,4,2,8,4,16]{0,5,3,2,1,4:T(8,128)(2,1)S(1)} %copy.29), channel_id=1, replica_groups=mesh['inp'=8,'tim'=4] {'tim'}, dimensions={4} | all-to-all | bytes 2097152 | tf_op jit(solution)/shard_map/all_to_all | solution.py:58
  118.5 15.4 %all-to-all-done.1 = bf16[128,16,2,8,1,16]{0,5,4,2,1,3:T(8,128)(2,1)S(1)} async-done(((bf16[128,16,2,8,1,16]{0,5,4,2,1,3:T(8,128)(2,1)}), bf16[128,16,2,8,1,16]{0,5,4,2,1,3:T(8,128)(2,1)S(1)}, u32[]{:S(2)}, u32[]{:S(2)}) %all-to-all-start.1) | async-done | bytes 1048608 | tf_op jit(solution)/shard_map/all_to_all | solution.py:57
  135.6 1305.0 %while.10 = (s32[]{:T(128)}, f32[16,528,2,1024]{3,2,1,0:T(2,128)}, bf16[16,2,1024,16]{2,0,1,3:T(8,128)(2,1)S(1)}, s32[528]{0:T(1024)S(1)}, s32[528]{0:T(1024)S(1)}, /*index=5*/s32[]{:T(128)}, s32[]{:T(128)}, s32[]{}) while((s32[]{:T(128)}, f32[16,528,2,1024]{3,2,1,0:T(2,128)}, bf16[16,2,1024,16]{2,0,1,3:T(8,128)(2,1)S(1)}, s32[528]{0:T(1024)S(1)}, ...), condition=%wide.region_1.2_spmd, body=%wide.region_0.1_spmd.sunk | while | flops 138958512 | bytes 60271528 | solution.py:86
  141.3 15.0 %maximum_multiply_fusion.2 = f32[32,32,2,32,32]{3,4,0,1,2:T(8,128)} fusion(f32[32,32,1,32,32]{3,4,0,1,2:T(8,128)S(1)} %convolution_bitcast_fusion.4, f32[32,32,1,32,32]{3,4,0,1,2:T(8,128)S(1)} %convolution_bitcast_fusion.5), kind=kLoop, calls=%fused_computation.1.clone.1 | loop fusion | flops 4194304 | bytes 16777216 | tf_op jit(solution)/shard_map/while/body/eval_jaxpr/mul | solution.py:82
  156.3 35.2 %gather_fusion = f32[528,2,32,32]{2,3,1,0:T(8,128)} fusion(f32[32,32,2,32,32]{3,4,0,1,2:T(8,128)} %maximum_multiply_fusion.2, s32[528]{0:T(1024)S(1)} %fusion.61), kind=kCustom, calls=%fused_computation.clone.1 | custom fusion | bytes 8654976 | tf_op jit(solution)/shard_map/while/body/eval_jaxpr/gather | solution.py:83
  191.5 12.4 copy.46
  203.9 7.7 copy.47
  222.8 15.0 %maximum_multiply_fusion.2 = f32[32,32,2,32,32]{3,4,0,1,2:T(8,128)} fusion(f32[32,32,1,32,32]{3,4,0,1,2:T(8,128)S(1)} %convolution_bitcast_fusion.4, f32[32,32,1,32,32]{3,4,0,1,2:T(8,128)S(1)} %convolution_bitcast_fusion.5), kind=kLoop, calls=%fused_computation.1.clone.1 | loop fusion | flops 4194304 | bytes 16777216 | tf_op jit(solution)/shard_map/while/body/eval_jaxpr/mul | solution.py:82
  237.8 35.2 %gather_fusion = f32[528,2,32,32]{2,3,1,0:T(8,128)} fusion(f32[32,32,2,32,32]{3,4,0,1,2:T(8,128)} %maximum_multiply_fusion.2, s32[528]{0:T(1024)S(1)} %fusion.61), kind=kCustom, calls=%fused_computation.clone.1 | custom fusion | bytes 8654976 | tf_op jit(solution)/shard_map/while/body/eval_jaxpr/gather | solution.py:83
  273.0 12.4 copy.46
  285.4 7.7 copy.47
  304.4 15.0 %maximum_multiply_fusion.2 = f32[32,32,2,32,32]{3,4,0,1,2:T(8,128)} fusion(f32[32,32,1,32,32]{3,4,0,1,2:T(8,128)S(1)} %convolution_bitcast_fusion.4, f32[32,32,1,32,32]{3,4,0,1,2:T(8,128)S(1)} %convolution_bitcast_fusion.5), kind=kLoop, calls=%fused_computation.1.clone.1 | loop fusion | flops 4194304 | bytes 16777216 | tf_op jit(solution)/shard_map/while/body/eval_jaxpr/mul | solution.py:82
  319.4 35.2 %gather_fusion = f32[528,2,32,32]{2,3,1,0:T(8,128)} fusion(f32[32,32,2,32,32]{3,4,0,1,2:T(8,128)} %maximum_multiply_fusion.2, s32[528]{0:T(1024)S(1)} %fusion.61), kind=kCustom, calls=%fused_computation.clone.1 | custom fusion | bytes 8654976 | tf_op jit(solution)/shard_map/while/body/eval_jaxpr/gather | solution.py:83
  354.6 12.4 copy.46
  367.0 7.7 copy.47
  385.9 15.0 %maximum_multiply_fusion.2 = f32[32,32,2,32,32]{3,4,0,1,2:T(8,128)} fusion(f32[32,32,1,32,32]{3,4,0,1,2:T(8,128)S(1)} %convolution_bitcast_fusion.4, f32[32,32,1,32,32]{3,4,0,1,2:T(8,128)S(1)} %convolution_bitcast_fusion.5), kind=kLoop, calls=%fused_computation.1.clone.1 | loop fusion | flops 4194304 | bytes 16777216 | tf_op jit(solution)/shard_map/while/body/eval_jaxpr/mul | solution.py:82
  400.9 35.2 %gather_fusion = f32[528,2,32,32]{2,3,1,0:T(8,128)} fusion(f32[32,32,2,32,32]{3,4,0,1,2:T(8,128)} %maximum_multiply_fusion.2, s32[528]{0:T(1024)S(1)} %fusion.61), kind=kCustom, calls=%fused_computation.clone.1 | custom fusion | bytes 8654976 | tf_op jit(solution)/shard_map/while/body/eval_jaxpr/gather | solution.py:83
  436.1 12.4 copy.46
  448.5 7.7 copy.47
  467.5 15.0 %maximum_multiply_fusion.2 = f32[32,32,2,32,32]{3,4,0,1,2:T(8,128)} fusion(f32[32,32,1,32,32]{3,4,0,1,2:T(8,128)S(1)} %convolution_bitcast_fusion.4, f32[32,32,1,32,32]{3,4,0,1,2:T(8,128)S(1)} %convolution_bitcast_fusion.5), kind=kLoop, calls=%fused_computation.1.clone.1 | loop fusion | flops 4194304 | bytes 16777216 | tf_op jit(solution)/shard_map/while/body/eval_jaxpr/mul | solution.py:82
  482.4 35.2 %gather_fusion = f32[528,2,32,32]{2,3,1,0:T(8,128)} fusion(f32[32,32,2,32,32]{3,4,0,1,2:T(8,128)} %maximum_multiply_fusion.2, s32[528]{0:T(1024)S(1)} %fusion.61), kind=kCustom, calls=%fused_computation.clone.1 | custom fusion | bytes 8654976 | tf_op jit(solution)/shard_map/while/body/eval_jaxpr/gather | solution.py:83
  517.7 12.4 copy.46
  530.1 7.7 copy.47
  549.0 15.0 %maximum_multiply_fusion.2 = f32[32,32,2,32,32]{3,4,0,1,2:T(8,128)} fusion(f32[32,32,1,32,32]{3,4,0,1,2:T(8,128)S(1)} %convolution_bitcast_fusion.4, f32[32,32,1,32,32]{3,4,0,1,2:T(8,128)S(1)} %convolution_bitcast_fusion.5), kind=kLoop, calls=%fused_computation.1.clone.1 | loop fusion | flops 4194304 | bytes 16777216 | tf_op jit(solution)/shard_map/while/body/eval_jaxpr/mul | solution.py:82
  564.0 35.2 %gather_fusion = f32[528,2,32,32]{2,3,1,0:T(8,128)} fusion(f32[32,32,2,32,32]{3,4,0,1,2:T(8,128)} %maximum_multiply_fusion.2, s32[528]{0:T(1024)S(1)} %fusion.61), kind=kCustom, calls=%fused_computation.clone.1 | custom fusion | bytes 8654976 | tf_op jit(solution)/shard_map/while/body/eval_jaxpr/gather | solution.py:83
  599.2 12.4 copy.46
  611.6 7.7 copy.47
  630.6 15.0 %maximum_multiply_fusion.2 = f32[32,32,2,32,32]{3,4,0,1,2:T(8,128)} fusion(f32[32,32,1,32,32]{3,4,0,1,2:T(8,128)S(1)} %convolution_bitcast_fusion.4, f32[32,32,1,32,32]{3,4,0,1,2:T(8,128)S(1)} %convolution_bitcast_fusion.5), kind=kLoop, calls=%fused_computation.1.clone.1 | loop fusion | flops 4194304 | bytes 16777216 | tf_op jit(solution)/shard_map/while/body/eval_jaxpr/mul | solution.py:82
  645.5 35.2 %gather_fusion = f32[528,2,32,32]{2,3,1,0:T(8,128)} fusion(f32[32,32,2,32,32]{3,4,0,1,2:T(8,128)} %maximum_multiply_fusion.2, s32[528]{0:T(1024)S(1)} %fusion.61), kind=kCustom, calls=%fused_computation.clone.1 | custom fusion | bytes 8654976 | tf_op jit(solution)/shard_map/while/body/eval_jaxpr/gather | solution.py:83
  680.8 12.4 copy.46
  693.2 7.7 copy.47
  712.1 15.0 %maximum_multiply_fusion.2 = f32[32,32,2,32,32]{3,4,0,1,2:T(8,128)} fusion(f32[32,32,1,32,32]{3,4,0,1,2:T(8,128)S(1)} %convolution_bitcast_fusion.4, f32[32,32,1,32,32]{3,4,0,1,2:T(8,128)S(1)} %convolution_bitcast_fusion.5), kind=kLoop, calls=%fused_computation.1.clone.1 | loop fusion | flops 4194304 | bytes 16777216 | tf_op jit(solution)/shard_map/while/body/eval_jaxpr/mul | solution.py:82
  727.1 35.2 %gather_fusion = f32[528,2,32,32]{2,3,1,0:T(8,128)} fusion(f32[32,32,2,32,32]{3,4,0,1,2:T(8,128)} %maximum_multiply_fusion.2, s32[528]{0:T(1024)S(1)} %fusion.61), kind=kCustom, calls=%fused_computation.clone.1 | custom fusion | bytes 8654976 | tf_op jit(solution)/shard_map/while/body/eval_jaxpr/gather | solution.py:83
  762.3 12.4 copy.46
  774.7 7.7 copy.47
  793.6 15.0 %maximum_multiply_fusion.2 = f32[32,32,2,32,32]{3,4,0,1,2:T(8,128)} fusion(f32[32,32,1,32,32]{3,4,0,1,2:T(8,128)S(1)} %convolution_bitcast_fusion.4, f32[32,32,1,32,32]{3,4,0,1,2:T(8,128)S(1)} %convolution_bitcast_fusion.5), kind=kLoop, calls=%fused_computation.1.clone.1 | loop fusion | flops 4194304 | bytes 16777216 | tf_op jit(solution)/shard_map/while/body/eval_jaxpr/mul | solution.py:82
  808.6 35.2 %gather_fusion = f32[528,2,32,32]{2,3,1,0:T(8,128)} fusion(f32[32,32,2,32,32]{3,4,0,1,2:T(8,128)} %maximum_multiply_fusion.2, s32[528]{0:T(1024)S(1)} %fusion.61), kind=kCustom, calls=%fused_computation.clone.1 | custom fusion | bytes 8654976 | tf_op jit(solution)/shard_map/while/body/eval_jaxpr/gather | solution.py:83
  843.9 12.4 copy.46
  856.3 7.7 copy.47
  875.2 15.0 %maximum_multiply_fusion.2 = f32[32,32,2,32,32]{3,4,0,1,2:T(8,128)} fusion(f32[32,32,1,32,32]{3,4,0,1,2:T(8,128)S(1)} %convolution_bitcast_fusion.4, f32[32,32,1,32,32]{3,4,0,1,2:T(8,128)S(1)} %convolution_bitcast_fusion.5), kind=kLoop, calls=%fused_computation.1.clone.1 | loop fusion | flops 4194304 | bytes 16777216 | tf_op jit(solution)/shard_map/while/body/eval_jaxpr/mul | solution.py:82
  890.2 35.2 %gather_fusion = f32[528,2,32,32]{2,3,1,0:T(8,128)} fusion(f32[32,32,2,32,32]{3,4,0,1,2:T(8,128)} %maximum_multiply_fusion.2, s32[528]{0:T(1024)S(1)} %fusion.61), kind=kCustom, calls=%fused_computation.clone.1 | custom fusion | bytes 8654976 | tf_op jit(solution)/shard_map/while/body/eval_jaxpr/gather | solution.py:83
  925.4 12.4 copy.46
  956.7 15.0 %maximum_multiply_fusion.2 = f32[32,32,2,32,32]{3,4,0,1,2:T(8,128)} fusion(f32[32,32,1,32,32]{3,4,0,1,2:T(8,128)S(1)} %convolution_bitcast_fusion.4, f32[32,32,1,32,32]{3,4,0,1,2:T(8,128)S(1)} %convolution_bitcast_fusion.5), kind=kLoop, calls=%fused_computation.1.clone.1 | loop fusion | flops 4194304 | bytes 16777216 | tf_op jit(solution)/shard_map/while/body/eval_jaxpr/mul | solution.py:82
  971.7 35.2 %gather_fusion = f32[528,2,32,32]{2,3,1,0:T(8,128)} fusion(f32[32,32,2,32,32]{3,4,0,1,2:T(8,128)} %maximum_multiply_fusion.2, s32[528]{0:T(1024)S(1)} %fusion.61), kind=kCustom, calls=%fused_computation.clone.1 | custom fusion | bytes 8654976 | tf_op jit(solution)/shard_map/while/body/eval_jaxpr/gather | solution.py:83
  1007.0 12.4 copy.46
  1038.3 15.0 %maximum_multiply_fusion.2 = f32[32,32,2,32,32]{3,4,0,1,2:T(8,128)} fusion(f32[32,32,1,32,32]{3,4,0,1,2:T(8,128)S(1)} %convolution_bitcast_fusion.4, f32[32,32,1,32,32]{3,4,0,1,2:T(8,128)S(1)} %convolution_bitcast_fusion.5), kind=kLoop, calls=%fused_computation.1.clone.1 | loop fusion | flops 4194304 | bytes 16777216 | tf_op jit(solution)/shard_map/while/body/eval_jaxpr/mul | solution.py:82
  1053.3 35.2 %gather_fusion = f32[528,2,32,32]{2,3,1,0:T(8,128)} fusion(f32[32,32,2,32,32]{3,4,0,1,2:T(8,128)} %maximum_multiply_fusion.2, s32[528]{0:T(1024)S(1)} %fusion.61), kind=kCustom, calls=%fused_computation.clone.1 | custom fusion | bytes 8654976 | tf_op jit(solution)/shard_map/while/body/eval_jaxpr/gather | solution.py:83
  1088.5 12.4 copy.46
  1119.8 15.0 %maximum_multiply_fusion.2 = f32[32,32,2,32,32]{3,4,0,1,2:T(8,128)} fusion(f32[32,32,1,32,32]{3,4,0,1,2:T(8,128)S(1)} %convolution_bitcast_fusion.4, f32[32,32,1,32,32]{3,4,0,1,2:T(8,128)S(1)} %convolution_bitcast_fusion.5), kind=kLoop, calls=%fused_computation.1.clone.1 | loop fusion | flops 4194304 | bytes 16777216 | tf_op jit(solution)/shard_map/while/body/eval_jaxpr/mul | solution.py:82
  1134.8 35.2 %gather_fusion = f32[528,2,32,32]{2,3,1,0:T(8,128)} fusion(f32[32,32,2,32,32]{3,4,0,1,2:T(8,128)} %maximum_multiply_fusion.2, s32[528]{0:T(1024)S(1)} %fusion.61), kind=kCustom, calls=%fused_computation.clone.1 | custom fusion | bytes 8654976 | tf_op jit(solution)/shard_map/while/body/eval_jaxpr/gather | solution.py:83
  1170.1 12.4 copy.46
  1201.4 15.0 %maximum_multiply_fusion.2 = f32[32,32,2,32,32]{3,4,0,1,2:T(8,128)} fusion(f32[32,32,1,32,32]{3,4,0,1,2:T(8,128)S(1)} %convolution_bitcast_fusion.4, f32[32,32,1,32,32]{3,4,0,1,2:T(8,128)S(1)} %convolution_bitcast_fusion.5), kind=kLoop, calls=%fused_computation.1.clone.1 | loop fusion | flops 4194304 | bytes 16777216 | tf_op jit(solution)/shard_map/while/body/eval_jaxpr/mul | solution.py:82
  1216.4 35.2 %gather_fusion = f32[528,2,32,32]{2,3,1,0:T(8,128)} fusion(f32[32,32,2,32,32]{3,4,0,1,2:T(8,128)} %maximum_multiply_fusion.2, s32[528]{0:T(1024)S(1)} %fusion.61), kind=kCustom, calls=%fused_computation.clone.1 | custom fusion | bytes 8654976 | tf_op jit(solution)/shard_map/while/body/eval_jaxpr/gather | solution.py:83
  1251.6 12.4 copy.46
  1282.9 15.0 %maximum_multiply_fusion.2 = f32[32,32,2,32,32]{3,4,0,1,2:T(8,128)} fusion(f32[32,32,1,32,32]{3,4,0,1,2:T(8,128)S(1)} %convolution_bitcast_fusion.4, f32[32,32,1,32,32]{3,4,0,1,2:T(8,128)S(1)} %convolution_bitcast_fusion.5), kind=kLoop, calls=%fused_computation.1.clone.1 | loop fusion | flops 4194304 | bytes 16777216 | tf_op jit(solution)/shard_map/while/body/eval_jaxpr/mul | solution.py:82
  1297.9 35.2 %gather_fusion = f32[528,2,32,32]{2,3,1,0:T(8,128)} fusion(f32[32,32,2,32,32]{3,4,0,1,2:T(8,128)} %maximum_multiply_fusion.2, s32[528]{0:T(1024)S(1)} %fusion.61), kind=kCustom, calls=%fused_computation.clone.1 | custom fusion | bytes 8654976 | tf_op jit(solution)/shard_map/while/body/eval_jaxpr/gather | solution.py:83
  1333.1 12.4 copy.46
  1364.5 15.0 %maximum_multiply_fusion.2 = f32[32,32,2,32,32]{3,4,0,1,2:T(8,128)} fusion(f32[32,32,1,32,32]{3,4,0,1,2:T(8,128)S(1)} %convolution_bitcast_fusion.4, f32[32,32,1,32,32]{3,4,0,1,2:T(8,128)S(1)} %convolution_bitcast_fusion.5), kind=kLoop, calls=%fused_computation.1.clone.1 | loop fusion | flops 4194304 | bytes 16777216 | tf_op jit(solution)/shard_map/while/body/eval_jaxpr/mul | solution.py:82
  1379.5 35.2 %gather_fusion = f32[528,2,32,32]{2,3,1,0:T(8,128)} fusion(f32[32,32,2,32,32]{3,4,0,1,2:T(8,128)} %maximum_multiply_fusion.2, s32[528]{0:T(1024)S(1)} %fusion.61), kind=kCustom, calls=%fused_computation.clone.1 | custom fusion | bytes 8654976 | tf_op jit(solution)/shard_map/while/body/eval_jaxpr/gather | solution.py:83
  1414.7 12.4 copy.46
  (166 shorter events, 278.6 us)
Async XLA Ops:
  2.0 21.7 %collective-permute-start = (bf16[2,128,3,512]{3,1,2,0:T(8,128)(2,1)S(1)}, bf16[2,128,3,512]{3,1,2,0:T(8,128)(2,1)S(1)}, u32[]{:S(2)}, u32[]{:S(2)}) collective-permute-start(bf16[2,128,3,512]{3,1,2,0:T(8,128)(2,1)S(1)} %copy.24), channel_id=1, source_target_pairs={{0,1},{1,2},{2,3},{4,5},{5,6},{6,7},{8,9},{9,10},{10,11},{12,13},{... | collective-permute-start | bytes 2359304 | tf_op jit(solution)/shard_map/ppermute | solution.py:15
  70.7 47.7 %copy-start = (s32[528,2]{0,1:T(2,128)S(1)}, s32[528,2]{0,1:T(2,128)}, u32[]{:S(2)}) copy-start(s32[528,2]{0,1:T(2,128)} %param.9) | copy-start | bytes 12676
  114.7 19.1 %all-to-all-start.1 = ((bf16[128,16,2,8,1,16]{0,5,4,2,1,3:T(8,128)(2,1)}), bf16[128,16,2,8,1,16]{0,5,4,2,1,3:T(8,128)(2,1)S(1)}, u32[]{:S(2)}, u32[]{:S(2)}) async-start(bf16[128,16,2,8,1,16]{0,5,4,2,1,3:T(8,128)(2,1)} %copy.30), calls=%async_computation.1 | async-start | bytes 2097152 | tf_op jit(solution)/shard_map/all_to_all | solution.py:57
where the time goes:
time: 1450 us; the launch traced here: 1440 us
  local copies, waits for them, and re-layouts  1010 us (70%)
  other arithmetic  252 us (17%)
  matrix products  104 us (7%)
  waiting for transfers between devices  30.5 us (2%)
  blocking collectives  30.4 us (2%)
    gather x32, local copies, waits for them, and re-layouts, one_channel(): picked = grid[first_index, second_index]  762 us
    mul x16, other arithmetic, one_channel(): grid = jnp.stack([real_grid, imag_grid], axis=2) * scale  239 us
    dynamic_update_slice x32, local copies, waits for them, and re-layouts, body(): return lax.map(one_channel, ordered)  216 us
    dot_general x16, matrix products, one_channel(): jnp.einsum('iuk,jvk->ijuv', right_side, right_side, preferred_element_typ...  38.9 us
    dot_general x16, matrix products, one_channel(): jnp.einsum('iuk,jvk->ijuv', turned, right_side, preferred_element_type=jn...  38.7 us
    all_to_all x1, blocking collectives, body(): lax.all_to_all(sectioned, 'tim', split_axis=4, concat_axis=1, tiled=True)  30.4 us
  transfers between devices with their start and end apart: 2, of which 2 were waited for; matrix products, arithmetic and copies ran while one was open for 0% of the time, Pallas kernels for 0%

commit v1 on v0

v1 whole, which is shorter than its diff:
```python
import functools
import math

import jax
import jax.numpy as jnp
import numpy as np
from jax import lax
from jax.experimental import pallas as pl
from jax.experimental.pallas import tpu as pltpu
from jax.sharding import PartitionSpec as P

TB = 32
FLAGRUN = 4
LANES = 128
PACK = LANES // TB
ROWS = TB // PACK


def shifted(block, axis, distance):
    devices = range(lax.axis_size(axis))
    route = [(i - distance, i) for i in devices if i - distance in devices]
    return lax.ppermute(block, axis, route)


def split_terms(value):
    high = value.astype(jnp.bfloat16)
    return high, (value - high.astype(jnp.float32)).astype(jnp.bfloat16)


def transform_tables(chans):
    radix = chans // LANES
    k = np.arange(LANES)
    tables = []
    for q in range(radix):
        phase = np.outer(radix * k + q, np.arange(LANES)) % chans
        angle = 2.0 * np.pi * phase / chans
        cosine, sine = np.cos(angle), np.sin(angle)
        tables.append(np.block([[cosine, sine], [-sine, cosine]]))
    table = np.stack(tables)
    high = table.astype(jnp.bfloat16)
    low = (table - high.astype(np.float64)).astype(jnp.bfloat16)
    return high, low


def channelize_kernel(volt_ref, halo_ref, taps_ref, flags_ref, high_ref, low_ref, out_ref, rows_ref, *, taps, chans):
    width = volt_ref.shape[1]
    spectra = volt_ref.shape[2] // chans
    radix = chans // LANES
    scale = 1.0 / (2048.0 * math.sqrt(taps * chans))
    coeffs = taps_ref[...].astype(jnp.float32) * scale

    def frame(part, index):
        if index < taps - 1:
            return halo_ref[part, :, index * chans : (index + 1) * chans].astype(jnp.float32)
        begin = (index - taps + 1) * chans
        return volt_ref[part, :, begin : begin + chans].astype(jnp.float32)

    folded = [[] for _ in range(radix)]
    for s in range(spectra):
        flag = flags_ref[:, s : s + 1]
        parts = []
        for part in range(2):
            total = coeffs[0:1] * frame(part, s + taps - 1)
            for p in range(1, taps):
                total = total + coeffs[p : p + 1] * frame(part, s + taps - 1 - p)
            total = total * flag
            parts.append([total[:, m * LANES : (m + 1) * LANES] for m in range(radix)])
        (r0, r1, r2, r3), (i0, i1, i2, i3) = parts
        re_even, re_odd, re_diff, re_cross = r0 + r2, r1 + r3, r0 - r2, r1 - r3
        im_even, im_odd, im_diff, im_cross = i0 + i2, i1 + i3, i0 - i2, i1 - i3
        sums = [
            (re_even + re_odd, im_even + im_odd),
            (re_diff + im_cross, im_diff - re_cross),
            (re_even - re_odd, im_even - im_odd),
            (re_diff - im_cross, im_diff + re_cross),
        ]
        for q in range(radix):
            folded[q].append(jnp.concatenate(sums[q], axis=1))
    nt = (((1,), (1,)), ((), ()))
    dot = functools.partial(lax.dot_general, dimension_numbers=nt, preferred_element_type=jnp.float32)
    for q in range(radix):
        high, low = split_terms(jnp.concatenate(folded[q], axis=0))
        result = dot(high_ref[q], high) + (dot(low_ref[q], high) + dot(high_ref[q], low))
        for part in range(2):
            for s in range(spectra):
                first = (q * 2 + part) * spectra + s
                rows_ref[pl.ds(first, LANES, stride=radix * 2 * spectra), :] = result[
                    part * LANES : (part + 1) * LANES, s * width : (s + 1) * width
                ]
    out_ref[...] = rows_ref[...].astype(jnp.bfloat16).reshape(out_ref.shape)


def channelize(voltages, halo, fir_taps, flags):
    taps, chans = fir_taps.shape
    width = voltages.shape[1]
    spectra = voltages.shape[2] // chans
    high, low = transform_tables(chans)
    return pl.pallas_call(
        functools.partial(channelize_kernel, taps=taps, chans=chans),
        out_shape=jax.ShapeDtypeStruct((chans, 2 * spectra, width), jnp.bfloat16),
        scratch_shapes=[pltpu.VMEM((chans * 2 * spectra, width), jnp.float32)],
        compiler_params=pltpu.CompilerParams(vmem_limit_bytes=40 << 20),
        name="channelize",
    )(voltages, halo, fir_taps, flags, jnp.asarray(high), jnp.asarray(low))


def correlate_kernel(place_ref, x_ref, pick_ref, spread_ref, out_ref, left_ref, right_ref, *, n_inputs, n_times):
    half = x_ref.shape[2] // 2
    width = x_ref.shape[3]
    depth = n_times * 2 * half
    deep = PACK * depth
    tiles = width // TB
    blocks = n_inputs * tiles
    row_block = lax.broadcasted_iota(jnp.int32, (deep, width), 0) // depth
    own = lax.broadcasted_iota(jnp.int32, (deep, width), 1) % PACK == row_block
    wide = tiles * LANES
    row_wide = lax.broadcasted_iota(jnp.int32, (deep, wide), 0) // depth
    own_wide = lax.broadcasted_iota(jnp.int32, (deep, wide), 1) // TB % PACK == row_wide
    sign = jnp.where(lax.broadcasted_iota(jnp.int32, (2 * half, width), 0) < half, 1.0, -1.0)
    zero = jnp.zeros((), jnp.float32)
    for i in range(n_inputs):
        plain, turned = [], []
        for t in range(n_times):
            value = x_ref[i * n_times + t, 0].astype(jnp.float32)
            plain.append(value)
            turned.append(pltpu.roll(value, half, 0) * sign)
        plain = jnp.concatenate(plain, axis=0)
        turned = jnp.concatenate(turned, axis=0)
        lefts = jnp.concatenate(
            [
                jnp.where(own, jnp.concatenate([plain] * PACK, axis=0), zero),
                jnp.where(own, jnp.concatenate([turned] * PACK, axis=0), zero),
            ],
            axis=1,
        ).astype(jnp.bfloat16)
        left = lax.dot_general(
            pick_ref[...], lefts, (((1,), (1,)), ((), ())), preferred_element_type=jnp.float32
        )
        span = tiles * ROWS * 2
        left_ref[i * span : (i + 1) * span, :] = left.astype(jnp.bfloat16)
        repeated = jnp.dot(plain.astype(jnp.bfloat16), spread_ref[...], preferred_element_type=jnp.float32)
        right = jnp.where(own_wide, jnp.concatenate([repeated] * PACK, axis=0), zero)
        right_ref[:, i * wide : (i + 1) * wide] = right.astype(jnp.bfloat16)
    tall = ROWS * 2
    for pair in range(blocks // 2):
        count = 2 * pair + 2
        grid = jnp.dot(
            left_ref[0 : count * tall, :],
            right_ref[:, pair * 2 * LANES : (pair + 1) * 2 * LANES],
            preferred_element_type=jnp.float32,
        )
        for first in range(count):
            for side in range(2):
                second = 2 * pair + side
                if first <= second:
                    out_ref[0, place_ref[first * blocks + second]] = grid[
                        first * tall : (first + 1) * tall, side * LANES : (side + 1) * LANES
                    ]


def correlate(owned, place, n_inputs, n_times, n_tiles):
    per_device, deep_half, width = owned.shape[1:]
    half = deep_half // 2
    tiles = width // TB
    blocks = n_inputs * tiles
    total = half * n_times
    tall = ROWS * 2
    row = np.arange(tiles * tall)
    column = np.arange(width)
    member = (row // 2)[:, None] == (column // PACK)[None, :]
    pick = np.concatenate([member & (row % 2 == q)[:, None] for q in range(2)], axis=1) / total
    lane = np.arange(tiles * LANES)
    spread = (lane // LANES * TB + lane % TB)[None, :] == column[:, None]
    deep = PACK * 2 * total
    grid_spec = pltpu.PrefetchScalarGridSpec(
        num_scalar_prefetch=1,
        grid=(per_device,),
        in_specs=[
            pl.BlockSpec((n_inputs * n_times, 1, deep_half, width), lambda r, place: (0, r, 0, 0)),
            pl.BlockSpec(pick.shape, lambda r, place: (0, 0)),
            pl.BlockSpec(spread.shape, lambda r, place: (0, 0)),
        ],
        out_specs=pl.BlockSpec((1, n_tiles, tall, LANES), lambda r, place: (r, 0, 0, 0)),
        scratch_shapes=[
            pltpu.VMEM((blocks * tall, deep), jnp.bfloat16),
            pltpu.VMEM((deep, blocks * LANES), jnp.bfloat16),
        ],
    )
    return pl.pallas_call(
        functools.partial(correlate_kernel, n_inputs=n_inputs, n_times=n_times),
        grid_spec=grid_spec,
        out_shape=jax.ShapeDtypeStruct((per_device, n_tiles, tall, LANES), jnp.float32),
        compiler_params=pltpu.CompilerParams(vmem_limit_bytes=48 << 20),
        name="correlate",
    )(place, owned, jnp.asarray(pick, jnp.bfloat16), jnp.asarray(spread, jnp.bfloat16))


def body(voltages, fir_taps, station_flags, tile_pairs):
    width = voltages.shape[1]
    taps_count, chans = fir_taps.shape
    local_spectra = voltages.shape[2] // chans
    n_inputs = lax.axis_size("inp")
    n_times = lax.axis_size("tim")
    devices = n_inputs * n_times
    halo = shifted(voltages[:, :, (local_spectra - taps_count + 1) * chans :], "tim", 1)
    flags = jnp.repeat(jnp.repeat(station_flags, 2, axis=0), FLAGRUN, axis=1).astype(jnp.float32)
    spectra = channelize(voltages, halo, fir_taps, flags)
    sectioned = spectra.reshape(devices, chans // devices, 2 * local_spectra, width)
    owned = lax.all_to_all(sectioned, ("inp", "tim"), 0, 0, tiled=True)
    blocks = width * n_inputs // TB
    n_tiles = tile_pairs.shape[0]
    code = tile_pairs[:, 0] * blocks + tile_pairs[:, 1]
    match = jnp.arange(blocks * blocks, dtype=jnp.int32)[:, None] == code[None, :]
    place = jnp.sum(jnp.where(match, jnp.arange(n_tiles, dtype=jnp.int32)[None, :], 0), axis=1)
    out = correlate(owned, place, n_inputs, n_times, n_tiles)
    per_device = chans // devices
    out = out.reshape(per_device, n_tiles, ROWS, 2, LANES)
    return jnp.transpose(out, (0, 1, 3, 2, 4)).reshape(per_device, n_tiles, 2, TB * TB)


def solution(mesh):
    in_specs = (P(None, "inp", "tim"), P(), P("inp", "tim"), P())
    out_specs = P(("inp", "tim"), None, None, None)
    return jax.shard_map(body, mesh=mesh, in_specs=in_specs, out_specs=out_specs, check_vma=False)
```

time: 1450 us -> 90.3 us (0.06)
  local copies, waits for them, and re-layouts: 1010 us -> 4.35 us
  other arithmetic: 252 us -> 0.97 us
  matrix products: 104 us -> 0 us
  Pallas kernels: 0 us -> 31.1 us
  blocking collectives: 30.4 us -> 0 us
    gather x32 -> x0, local copies, waits for them, and re-layouts: 762 us -> none  [one_channel(): picked = grid[first_index, second_index]]
    mul x18 -> x0, other arithmetic: 249 us -> none  [the longest x16 239 us: one_channel(): grid = jnp.stack([real_grid, imag_grid], axis=2) * scale]
    dynamic_update_slice x32 -> x0, local copies, waits for them, and re-layouts: 216 us -> none  [body(): return lax.map(one_channel, ordered)]
    dot_general x36 -> x0, matrix products: 104 us -> none  [the longest x16 38.9 us: one_channel(): jnp.einsum('iuk,jvk->ijuv', right_side, right_side, preferred_element_typ...]
    pallas_call x0 -> x2, Pallas kernels: none -> 31.1 us  [the longest x1 27.2 us: correlate(): pl.pallas_call(functools.partial(correlate_kernel, n_inputs=n_inputs, n_t...]
    all_to_all x1 -> x0, blocking collectives: 30.4 us -> none  [body(): lax.all_to_all(sectioned, 'tim', split_axis=4, concat_axis=1, tiled=True)]
  transfers between devices with their start and end apart: 2 -> 2, of which waited for: 2 -> 2; matrix products, arithmetic and copies ran while one was open for 0% -> 1% of each run, Pallas kernels for 0% -> 0%
where the time goes in v1:
time: 90.3 us; the launch traced here: 88.8 us
  waiting for transfers between devices  40.6 us (45%)
  Pallas kernels  31.1 us (34%)
  starting transfers between devices  11.7 us (13%)
  local copies, waits for them, and re-layouts  4.35 us (5%)
  other arithmetic  0.97 us (1%)
    pallas_call x1, Pallas kernels, correlate(): pl.pallas_call(functools.partial(correlate_kernel, n_inputs=n_inputs, n_t...  27.2 us
    all_to_all x1, waiting for transfers between devices, body(): owned = lax.all_to_all(sectioned, ('inp', 'tim'), 0, 0, tiled=True)  24.7 us
    ppermute x1, waiting for transfers between devices, shifted(): return lax.ppermute(block, axis, route)  15.9 us
    all_to_all x1, starting transfers between devices, body(): owned = lax.all_to_all(sectioned, ('inp', 'tim'), 0, 0, tiled=True)  6.75 us
    ppermute x1, starting transfers between devices, shifted(): return lax.ppermute(block, axis, route)  4.98 us
    pallas_call x1, Pallas kernels, channelize(): pl.pallas_call(functools.partial(channelize_kernel, taps=taps, chans=chan...  3.89 us
    unnamed x14, local copies, waits for them, and re-layouts  2.79 us
  transfers between devices with their start and end apart: 2, of which 2 were waited for; matrix products, arithmetic and copies ran while one was open for 1% of the time, Pallas kernels for 0%

profile of v1, /device:TPU:0, one launch (start us, length us, event | category | flops | bytes accessed | tf_op | source)
XLA Modules:
  0.0 88.8 jit_solution(3376165006628381576)
XLA Ops:
  0.0 0.0 copy-start
  0.0 1.3 %slice.11 = bf16[2,128,1536]{2,1,0:T(8,128)(2,1)S(1)} slice(bf16[2,128,2048]{2,1,0:T(8,128)(2,1)} %volt_ref.1), slice={[0:2], [0:128], [512:2048]} | slice | bytes 1572864 | tf_op jit(solution)/shard_map/slice | solution.py:205
  1.3 5.0 %collective-permute-start = (bf16[2,128,1536]{2,1,0:T(8,128)(2,1)S(1)}, bf16[2,128,1536]{2,1,0:T(8,128)(2,1)S(1)}, u32[]{:S(2)}, u32[]{:S(2)}) collective-permute-start(bf16[2,128,1536]{2,1,0:T(8,128)(2,1)S(1)} %slice.11), channel_id=1, source_target_pairs={{0,1},{1,2},{2,3},{4,5},{5,6},{6,7},{8,9},{9,10},{10,11},{12,13},{... | collective-permute-start | bytes 2359304 | tf_op jit(solution)/shard_map/ppermute | solution.py:22
  6.3 0.7 convert_bitcast_fusion
  6.9 0.1 broadcast_in_dim.21
  7.0 0.1 convert_element_type.9
  7.1 15.9 %collective-permute-done.halo_ref = bf16[2,128,1536]{2,1,0:T(8,128)(2,1)S(1)} collective-permute-done((bf16[2,128,1536]{2,1,0:T(8,128)(2,1)S(1)}, bf16[2,128,1536]{2,1,0:T(8,128)(2,1)S(1)}, u32[]{:S(2)}, u32[]{:S(2)}) %collective-permute-start) | collective-permute-done | bytes 786464 | tf_op jit(solution)/shard_map/ppermute | solution.py:22
  23.0 0.1 reshape.32.flags_ref
  23.1 0.0 copy-done
  23.1 0.0 copy-start.1
  23.1 1.0 %copy-done.1 = bf16[4,256,256]{2,1,0:T(8,128)(2,1)S(1)} copy-done((bf16[4,256,256]{2,1,0:T(8,128)(2,1)S(1)}, bf16[4,256,256]{2,1,0:T(8,128)(2,1)}, u32[]{:S(2)}) %copy-start.1) | copy-done | bytes 524312
  24.1 0.0 copy-start.2
  24.1 1.0 %copy-done.2 = bf16[4,256,256]{2,1,0:T(8,128)(2,1)S(1)} copy-done((bf16[4,256,256]{2,1,0:T(8,128)(2,1)S(1)}, bf16[4,256,256]{2,1,0:T(8,128)(2,1)}, u32[]{:S(2)}) %copy-start.2) | copy-done | bytes 524312
  25.2 0.0 copy-start.5
  25.2 0.7 copy-done.5
  25.9 0.0 copy-start.6
  25.9 0.0 copy-start.3
  25.9 0.0 copy-start.4
  25.9 3.9 %channelize.1 = bf16[512,8,128]{2,1,0:T(8,128)(2,1)} custom-call(bf16[2,128,2048]{2,1,0:T(8,128)(2,1)S(1)} %copy-done, bf16[2,128,1536]{2,1,0:T(8,128)(2,1)S(1)} %collective-permute-done.halo_ref, s32[4,512]{1,0:T(4,128)S(1)} %copy-done.5, f32[128,4]{1,0:T(8,128)S(1)} %reshape.32.flags_ref, bf16[4,256,256]{2,1,0:T(8,128)(2,1)S(1)} %copy-done.2, ...), custom_call_target="tpu_custom_call" | custom-call | tf_op jit(solution)/shard_map/channelize/pallas_call | solution.py:98
  29.8 6.8 %all-to-all-start = ((bf16[32,16,8,128]{3,2,1,0:T(8,128)(2,1)}), bf16[32,16,8,128]{3,2,1,0:T(8,128)(2,1)S(1)}, u32[]{:S(2)}, u32[]{:S(2)}) async-start(bf16[32,16,8,128]{3,2,1,0:T(8,128)(2,1)} %bitcast.1), calls=%async_computation | async-start | bytes 2097152 | tf_op jit(solution)/shard_map/all_to_all | solution.py:209
  36.5 0.0 copy-done.6
  36.6 0.3 select_reduce_fusion.place_ref
  36.9 24.7 %all-to-all-done.x_ref = bf16[32,16,8,128]{3,2,1,0:T(8,128)(2,1)S(1)} async-done(((bf16[32,16,8,128]{3,2,1,0:T(8,128)(2,1)}), bf16[32,16,8,128]{3,2,1,0:T(8,128)(2,1)S(1)}, u32[]{:S(2)}, u32[]{:S(2)}) %all-to-all-start) | async-done | bytes 1048608 | tf_op jit(solution)/shard_map/all_to_all | solution.py:209
  61.6 0.0 copy-done.3
  61.6 0.0 copy-done.4
  61.6 27.2 %correlate.1 = f32[16,528,16,128]{3,2,1,0:T(8,128)} custom-call(s32[1024]{0:T(1024)S(1)} %select_reduce_fusion.place_ref, bf16[32,16,8,128]{3,2,1,0:T(8,128)(2,1)S(1)} %all-to-all-done.x_ref, bf16[64,256]{1,0:T(8,128)(2,1)S(1)} %copy-done.4, bf16[128,512]{1,0:T(8,128)(2,1)S(1)} %copy-done.3), custom_call_target="tpu_custom_call" | custom-call | tf_op jit(solution)/shard_map/correlate/pallas_call | solution.py:189
  (1 shorter events, 0.0 us)
Async XLA Ops:
  0.0 23.1 %copy-start = (bf16[2,128,2048]{2,1,0:T(8,128)(2,1)S(1)}, bf16[2,128,2048]{2,1,0:T(8,128)(2,1)}, u32[]{:S(2)}) copy-start(bf16[2,128,2048]{2,1,0:T(8,128)(2,1)} %volt_ref.1) | copy-start | bytes 3145732
  1.3 21.7 %collective-permute-start = (bf16[2,128,1536]{2,1,0:T(8,128)(2,1)S(1)}, bf16[2,128,1536]{2,1,0:T(8,128)(2,1)S(1)}, u32[]{:S(2)}, u32[]{:S(2)}) collective-permute-start(bf16[2,128,1536]{2,1,0:T(8,128)(2,1)S(1)} %slice.11), channel_id=1, source_target_pairs={{0,1},{1,2},{2,3},{4,5},{5,6},{6,7},{8,9},{9,10},{10,11},{12,13},{... | collective-permute-start | bytes 2359304 | tf_op jit(solution)/shard_map/ppermute | solution.py:22
  23.1 1.0 %copy-start.1 = (bf16[4,256,256]{2,1,0:T(8,128)(2,1)S(1)}, bf16[4,256,256]{2,1,0:T(8,128)(2,1)}, u32[]{:S(2)}) copy-start(bf16[4,256,256]{2,1,0:T(8,128)(2,1)} %constant.13.clone.low_ref) | copy-start | bytes 1572868
  24.1 1.0 %copy-start.2 = (bf16[4,256,256]{2,1,0:T(8,128)(2,1)S(1)}, bf16[4,256,256]{2,1,0:T(8,128)(2,1)}, u32[]{:S(2)}) copy-start(bf16[4,256,256]{2,1,0:T(8,128)(2,1)} %constant.12.clone.high_ref) | copy-start | bytes 1572868
  25.2 0.7 copy-start.5
  25.9 10.7 %copy-start.6 = (s32[528,2]{0,1:T(2,128)S(1)}, s32[528,2]{0,1:T(2,128)}, u32[]{:S(2)}) copy-start(s32[528,2]{0,1:T(2,128)} %param.11) | copy-start | bytes 12676
  25.9 35.7 %copy-start.3 = (bf16[128,512]{1,0:T(8,128)(2,1)S(1)}, bf16[128,512]{1,0:T(8,128)(2,1)}, u32[]{:S(2)}) copy-start(bf16[128,512]{1,0:T(8,128)(2,1)} %constant.15.clone.spread_ref) | copy-start | bytes 393220
  25.9 35.7 %copy-start.4 = (bf16[64,256]{1,0:T(8,128)(2,1)S(1)}, bf16[64,256]{1,0:T(8,128)(2,1)}, u32[]{:S(2)}) copy-start(bf16[64,256]{1,0:T(8,128)(2,1)} %constant.14.clone.pick_ref) | copy-start | bytes 98308
  29.8 31.8 %all-to-all-start = ((bf16[32,16,8,128]{3,2,1,0:T(8,128)(2,1)}), bf16[32,16,8,128]{3,2,1,0:T(8,128)(2,1)S(1)}, u32[]{:S(2)}, u32[]{:S(2)}) async-start(bf16[32,16,8,128]{3,2,1,0:T(8,128)(2,1)} %bitcast.1), calls=%async_computation | async-start | bytes 2097152 | tf_op jit(solution)/shard_map/all_to_all | solution.py:209

commit v2 on v1

v2 whole, which is shorter than its diff:
```python
import functools
import math

import jax
import jax.numpy as jnp
import numpy as np
from jax import lax
from jax.experimental import pallas as pl
from jax.experimental.pallas import tpu as pltpu
from jax.sharding import PartitionSpec as P

TB = 32
FLAGRUN = 4
LANES = 128
PACK = LANES // TB
ROWS = TB // PACK


def shifted(block, axis, distance):
    devices = range(lax.axis_size(axis))
    route = [(i - distance, i) for i in devices if i - distance in devices]
    return lax.ppermute(block, axis, route)


def split_terms(value):
    high = value.astype(jnp.bfloat16)
    return high, (value - high.astype(jnp.float32)).astype(jnp.bfloat16)


def transform_tables(chans):
    radix = chans // LANES
    tables = []
    for q in range(radix):
        phase = np.outer(radix * np.arange(LANES) + q, np.arange(LANES)) % chans
        angle = 2.0 * np.pi * phase / chans
        cosine, sine = np.cos(angle), np.sin(angle)
        real = np.concatenate([cosine, sine], axis=1)
        imag = np.concatenate([-sine, cosine], axis=1)
        tables.append(np.stack([real, imag], axis=1).reshape(2 * LANES, 2 * LANES))
    table = np.stack(tables)
    high = table.astype(jnp.bfloat16)
    low = (table - high.astype(np.float64)).astype(jnp.bfloat16)
    return np.stack([high, low])


def channelize_kernel(*refs, taps, chans, first, count, n_halos, groups, n_started):
    volt_ref = refs[0]
    halo_refs = refs[1 : 1 + n_halos]
    taps_ref, flags_ref, table_ref = refs[1 + n_halos : 4 + n_halos]
    started_refs = refs[4 + n_halos : 4 + n_halos + n_started]
    out_refs = refs[4 + n_halos + n_started :]
    width = volt_ref.shape[1]
    radix = chans // LANES
    scale = 1.0 / (2048.0 * math.sqrt(taps * chans))
    coeffs = taps_ref[...].astype(jnp.float32) * scale

    def frame(part, index):
        ref, slot = volt_ref, index
        for halo_ref in halo_refs:
            if slot < 0:
                ref, slot = halo_ref, slot + halo_ref.shape[2] // chans
        return ref[part, :, slot * chans : (slot + 1) * chans].astype(jnp.float32)

    folded = [[] for _ in range(radix)]
    for s in range(first, first + count):
        flag = flags_ref[:, s : s + 1]
        parts = []
        for part in range(2):
            total = coeffs[0:1] * frame(part, s)
            for p in range(1, taps):
                total = total + coeffs[p : p + 1] * frame(part, s - p)
            total = total * flag
            parts.append([total[:, m * LANES : (m + 1) * LANES] for m in range(radix)])
        (r0, r1, r2, r3), (i0, i1, i2, i3) = parts
        re_even, re_odd, re_diff, re_cross = r0 + r2, r1 + r3, r0 - r2, r1 - r3
        im_even, im_odd, im_diff, im_cross = i0 + i2, i1 + i3, i0 - i2, i1 - i3
        sums = [
            (re_even + re_odd, im_even + im_odd),
            (re_diff + im_cross, im_diff - re_cross),
            (re_even - re_odd, im_even - im_odd),
            (re_diff - im_cross, im_diff + re_cross),
        ]
        for q in range(radix):
            folded[q].append(jnp.concatenate(sums[q], axis=1))
    nt = (((1,), (1,)), ((), ()))
    dot = functools.partial(lax.dot_general, dimension_numbers=nt, preferred_element_type=jnp.float32)
    spread, lanes = out_refs[0].shape[1], width
    for q in range(radix):
        high, low = split_terms(jnp.concatenate(folded[q], axis=0))
        result = dot(table_ref[0, q], high) + (dot(table_ref[1, q], high) + dot(table_ref[0, q], low))
        result = result.astype(jnp.bfloat16)
        owner, slot = divmod(q, radix // spread)
        for out_ref, group in zip(out_refs, groups):
            if 0 <= slot < group:
                for s in range(count):
                    piece = result[:, s * lanes : (s + 1) * lanes]
                    out_ref[:, owner, slot, s] = piece.reshape(out_ref.shape[0], out_ref.shape[4], lanes)
            slot -= group
    for out_ref, started_ref in zip(out_refs, started_refs):
        out_ref[:, :, :, count:] = started_ref[...]


def channel_plan(chans, devices):
    radix = chans // LANES
    per_device = chans // devices
    residues = min(per_device, radix)
    return residues, per_device // residues, radix // residues


def channelize(voltages, halos, fir_taps, flags, first, count, groups, devices, started):
    taps, chans = fir_taps.shape
    width = voltages.shape[1]
    spectra = count + sum(part.shape[3] for part in started[:1])
    _, strip, sharers = channel_plan(chans, devices)
    table = transform_tables(chans)
    return pl.pallas_call(
        functools.partial(
            channelize_kernel,
            taps=taps,
            chans=chans,
            first=first,
            count=count,
            n_halos=len(halos),
            groups=tuple(groups),
            n_started=len(started),
        ),
        out_shape=[
            jax.ShapeDtypeStruct((devices // sharers, sharers, group, spectra, 2 * strip, width), jnp.bfloat16)
            for group in groups
        ],
        compiler_params=pltpu.CompilerParams(vmem_limit_bytes=40 << 20),
        name="channelize",
    )(voltages, *halos, fir_taps, flags, jnp.asarray(table), *started)


def correlate_kernel(*refs, n_inputs, n_times, firsts, begin, residues, n_earlier):
    place_ref = refs[0]
    x_refs = refs[1 : 1 + len(firsts)]
    pick_ref, spread_ref = refs[1 + len(firsts) : 3 + len(firsts)]
    out_ref, rows_ref, *buffers, sems = refs[3 + len(firsts) + n_earlier :]
    slots = [buffers[at : at + 3] for at in range(0, len(buffers), 3)]
    _, group, _, double, width = x_refs[0].shape
    strip = double // 2
    channels = group * strip
    spectra = sum(x_ref.shape[2] for x_ref in x_refs)
    half = n_times * spectra
    depth = 2 * half
    tiles = width // TB
    blocks = n_inputs * tiles
    tall = ROWS * 2
    wide = tiles * LANES
    span = tiles * tall
    zero = jnp.zeros((), jnp.bfloat16)
    lane = lax.broadcasted_iota(jnp.int32, (depth, width), 1) % PACK
    lane_wide = lax.broadcasted_iota(jnp.int32, (depth, wide), 1) // TB % PACK

    def unpack(i):
        for t in range(n_times):
            for x_ref, first in zip(x_refs, firsts):
                for q in range(group):
                    for s in range(x_ref.shape[2]):
                        row = q * strip * depth + t * spectra + first + s
                        value = x_ref[i * n_times + t, q, s].astype(jnp.float32)
                        rows_ref[i, pl.ds(row, double, stride=half), :] = value

    def prepare(channel, slot, i):
        left_ref, right_ref, _ = slots[slot]
        plain = rows_ref[i, pl.ds(pl.multiple_of(channel * depth, depth), depth), :]
        turned = jnp.concatenate([plain[half:], -plain[:half]], axis=0).astype(jnp.bfloat16)
        plain = plain.astype(jnp.bfloat16)
        lefts = [
            jnp.concatenate([jnp.where(lane == u, value, zero) for u in range(PACK)], axis=0)
            for value in (plain, turned)
        ]
        left = lax.dot_general(
            pick_ref[...],
            jnp.concatenate(lefts, axis=1),
            (((1,), (1,)), ((), ())),
            preferred_element_type=jnp.float32,
        )
        left_ref[i * span : (i + 1) * span, :] = left.astype(jnp.bfloat16)
        right = jnp.dot(plain, spread_ref[...], preferred_element_type=jnp.float32).astype(jnp.bfloat16)
        for u in range(PACK):
            right_ref[u * depth : (u + 1) * depth, i * wide : (i + 1) * wide] = jnp.where(
                lane_wide == u, right, zero
            )

    def multiply(slot, pair):
        left_ref, right_ref, tile_ref = slots[slot]
        count = 2 * pair + 2
        grid = jnp.dot(
            left_ref[0 : count * tall, :],
            right_ref[:, pair * 2 * LANES : (pair + 1) * 2 * LANES],
            preferred_element_type=jnp.float32,
        )
        for first in range(count):
            for side in range(2):
                second = 2 * pair + side
                if first <= second:
                    tile_ref[place_ref[first * blocks + second]] = grid[
                        first * tall : (first + 1) * tall, side * LANES : (side + 1) * LANES
                    ]

    def store(channel, slot):
        target = channel % strip * residues + begin + channel // strip
        return pltpu.make_async_copy(slots[slot][2], out_ref.at[target], sems.at[slot])

    for i in range(n_inputs):
        unpack(i)
        prepare(0, 0, i)

    def advance(index, carry):
        for slot in range(len(slots)):
            channel = index * len(slots) + slot
            upcoming = jnp.minimum(channel + 1, channels - 1)

            @pl.when(index > 0)
            def _():
                store(channel - len(slots), slot).wait()

            ahead = [functools.partial(prepare, upcoming, (slot + 1) % len(slots), i) for i in range(n_inputs)]
            pairs = blocks // 2
            if len(slots) == 1 and channels > 1:
                for i in range(n_inputs):
                    prepare(channel, slot, i)
            for pair in range(pairs):
                multiply(slot, pair)
                if len(slots) > 1:
                    for task in ahead[pair * n_inputs // pairs : (pair + 1) * n_inputs // pairs]:
                        task()
            store(channel, slot).start()
        return carry

    rounds = channels // len(slots)
    lax.fori_loop(0, rounds, advance, 0)
    for slot in range(len(slots)):
        store(channels - len(slots) + slot, slot).wait()


def correlate(parts, firsts, place, begin, per_device, residues, n_inputs, n_times, n_tiles, filled):
    _, group, _, double, width = parts[0].shape
    channels = group * double // 2
    total = sum(part.shape[2] for part in parts) * n_times
    tiles = width // TB
    blocks = n_inputs * tiles
    tall = ROWS * 2
    row = np.arange(tiles * tall)
    column = np.arange(width)
    member = (row // 2)[:, None] == (column // PACK)[None, :]
    pick = np.concatenate([member & (row % 2 == q)[:, None] for q in range(2)], axis=1) / total
    lane = np.arange(tiles * LANES)
    spread = (lane // LANES * TB + lane % TB)[None, :] == column[:, None]
    deep = PACK * 2 * total
    earlier = [] if filled is None else [filled]
    slots = 2 if channels % 2 == 0 else 1
    in_vmem = pl.BlockSpec(memory_space=pltpu.VMEM)
    return pl.pallas_call(
        functools.partial(
            correlate_kernel,
            n_inputs=n_inputs,
            n_times=n_times,
            firsts=tuple(firsts),
            begin=begin,
            residues=residues,
            n_earlier=len(earlier),
        ),
        in_specs=[pl.BlockSpec(memory_space=pltpu.SMEM)]
        + [in_vmem] * (len(parts) + 2)
        + [pl.BlockSpec(memory_space=pl.ANY)] * len(earlier),
        out_specs=pl.BlockSpec(memory_space=pl.ANY),
        out_shape=jax.ShapeDtypeStruct((per_device, n_tiles, tall, LANES), jnp.float32),
        scratch_shapes=[pltpu.VMEM((n_inputs, channels * 2 * total, width), jnp.float32)]
        + [
            pltpu.VMEM((blocks * tall, deep), jnp.bfloat16),
            pltpu.VMEM((deep, blocks * LANES), jnp.bfloat16),
            pltpu.VMEM((n_tiles, tall, LANES), jnp.float32),
        ]
        * slots
        + [pltpu.SemaphoreType.DMA((slots,))],
        input_output_aliases={3 + len(parts): 0} if earlier else {},
        compiler_params=pltpu.CompilerParams(vmem_limit_bytes=48 << 20),
        name="correlate",
    )(place, *parts, jnp.asarray(pick, jnp.bfloat16), jnp.asarray(spread, jnp.bfloat16), *earlier)


def body(voltages, fir_taps, station_flags, tile_pairs):
    width = voltages.shape[1]
    taps, chans = fir_taps.shape
    spectra = voltages.shape[2] // chans
    n_inputs = lax.axis_size("inp")
    n_times = lax.axis_size("tim")
    devices = n_inputs * n_times
    per_device = chans // devices
    residues, _, _ = channel_plan(chans, devices)
    halo = shifted(voltages[:, :, (spectra - taps + 1) * chans :], "tim", 1)
    flags = jnp.repeat(jnp.repeat(station_flags, 2, axis=0), FLAGRUN, axis=1).astype(jnp.float32)
    exchange = functools.partial(lax.all_to_all, axis_name=("inp", "tim"), split_axis=0, concat_axis=0, tiled=True)
    groups = [residues // 2, residues - residues // 2] if residues > 1 else [residues]
    blocks = width * n_inputs // TB
    n_tiles = tile_pairs.shape[0]
    code = tile_pairs[:, 0] * blocks + tile_pairs[:, 1]
    match = jnp.arange(blocks * blocks, dtype=jnp.int32)[:, None] == code[None, :]
    place = jnp.sum(jnp.where(match, jnp.arange(n_tiles, dtype=jnp.int32)[None, :], 0), axis=1)
    own = taps - 1
    started = channelize(voltages, [], fir_taps, flags, own, spectra - own, groups, devices, [])
    spectra_groups = channelize(voltages, [halo], fir_taps, flags, 0, own, groups, devices, started)
    owned = [exchange(part.reshape((devices,) + part.shape[2:])) for part in spectra_groups]
    out, begin = None, 0
    for part, group in zip(owned, groups):
        out = correlate([part], [0], place, begin, per_device, residues, n_inputs, n_times, n_tiles, out)
        begin += group
    out = out.reshape(per_device, n_tiles, ROWS, 2, LANES)
    return jnp.transpose(out, (0, 1, 3, 2, 4)).reshape(per_device, n_tiles, 2, TB * TB)


def solution(mesh):
    in_specs = (P(None, "inp", "tim"), P(), P("inp", "tim"), P())
    out_specs = P(("inp", "tim"), None, None, None)
    return jax.shard_map(body, mesh=mesh, in_specs=in_specs, out_specs=out_specs, check_vma=False)
```

time: 90.3 us -> 81 us (0.90); the launches traced: 88.8 us -> 80.6 us
  waiting for transfers between devices: 40.6 us -> 13 us
  blocking collectives: 0 us -> 20.9 us
  starting transfers between devices: 11.7 us -> 9.06 us
  Pallas kernels: 31.1 us -> 33.1 us
    all_to_all x1, waiting for transfers between devices: 24.7 us -> 0.01 us  [body(): exchange(part.reshape((devices,) + part.shape[2:]))]
    all_to_all x0 -> x1, blocking collectives: none -> 20.9 us  [body(): exchange(part.reshape((devices,) + part.shape[2:]))]
    ppermute x1, waiting for transfers between devices: 15.9 us -> 13 us  [shifted(): return lax.ppermute(block, axis, route)]
    all_to_all x1, starting transfers between devices: 6.75 us -> 4.08 us  [body(): exchange(part.reshape((devices,) + part.shape[2:]))]
    pallas_call x1 -> x2, Pallas kernels: 27.2 us -> 29.9 us  [correlate(): pl.pallas_call(functools.partial(correlate_kernel, n_inputs=n_inputs, n_t...]
    unnamed x14 -> x12, local copies, waits for them, and re-layouts: 2.79 us -> 1.94 us
    pallas_call x1 -> x2, Pallas kernels: 3.89 us -> 3.16 us  [channelize(): pl.pallas_call(functools.partial(channelize_kernel, taps=taps, chans=chan...]
  transfers between devices with their start and end apart: 2 -> 2, of which waited for: 2 -> 1; matrix products, arithmetic and copies ran while one was open for 1% -> 2% of each run, Pallas kernels for 0% -> 20%
where the time goes in v2:
time: 81 us; the launch traced here: 80.6 us
  Pallas kernels  33.1 us (41%)
  blocking collectives  20.9 us (26%)
  waiting for transfers between devices  13 us (16%)
  starting transfers between devices  9.06 us (11%)
  local copies, waits for them, and re-layouts  3.5 us (4%)
  other arithmetic  0.97 us (1%)
    pallas_call x2, Pallas kernels, correlate(): pl.pallas_call(functools.partial(correlate_kernel, n_inputs=n_inputs, n_t...  29.9 us
    all_to_all x1, blocking collectives, body(): exchange(part.reshape((devices,) + part.shape[2:]))  20.9 us
    ppermute x1, waiting for transfers between devices, shifted(): return lax.ppermute(block, axis, route)  13 us
    ppermute x1, starting transfers between devices, shifted(): return lax.ppermute(block, axis, route)  4.98 us
    all_to_all x1, starting transfers between devices, body(): exchange(part.reshape((devices,) + part.shape[2:]))  4.08 us
    pallas_call x2, Pallas kernels, channelize(): pl.pallas_call(functools.partial(channelize_kernel, taps=taps, chans=chan...  3.16 us
    unnamed x12, local copies, waits for them, and re-layouts  1.94 us
  transfers between devices with their start and end apart: 2, of which 1 were waited for; matrix products, arithmetic and copies ran while one was open for 2% of the time, Pallas kernels for 20%

profile of v2, /device:TPU:0, one launch (start us, length us, event | category | flops | bytes accessed | tf_op | source)
XLA Modules:
  0.0 80.6 jit_solution(910146425824823139)
XLA Ops:
  0.0 0.0 copy-start
  0.0 1.3 %slice.11 = bf16[2,128,1536]{2,1,0:T(8,128)(2,1)S(1)} slice(bf16[2,128,2048]{2,1,0:T(8,128)(2,1)} %refs_0_.3), slice={[0:2], [0:128], [512:2048]} | slice | bytes 1572864 | tf_op jit(solution)/shard_map/slice | solution.py:295
  1.3 5.0 %collective-permute-start = (bf16[2,128,1536]{2,1,0:T(8,128)(2,1)S(1)}, bf16[2,128,1536]{2,1,0:T(8,128)(2,1)S(1)}, u32[]{:S(2)}, u32[]{:S(2)}) collective-permute-start(bf16[2,128,1536]{2,1,0:T(8,128)(2,1)S(1)} %slice.11), channel_id=1, source_target_pairs={{0,1},{1,2},{2,3},{4,5},{5,6},{6,7},{8,9},{9,10},{10,11},{12,13},{... | collective-permute-start | bytes 2359304 | tf_op jit(solution)/shard_map/ppermute | solution.py:22
  6.3 0.7 convert_bitcast_fusion
  6.9 0.1 broadcast_in_dim.21
  7.0 0.1 convert_element_type.9
  7.1 0.1 reshape.35.refs_2_.refs_3_
  7.2 0.0 copy-done
  7.2 0.0 copy-start.1
  7.2 1.2 %copy-done.1 = bf16[2,4,256,256]{3,2,1,0:T(8,128)(2,1)S(1)} copy-done((bf16[2,4,256,256]{3,2,1,0:T(8,128)(2,1)S(1)}, bf16[2,4,256,256]{3,2,1,0:T(8,128)(2,1)}, u32[]{:S(2)}) %copy-start.1) | copy-done | bytes 1048600
  8.5 0.0 copy-start.4
  8.5 0.7 copy-done.4
  9.2 0.8 channelize.2
  10.0 13.0 %collective-permute-done.refs_1_ = bf16[2,128,1536]{2,1,0:T(8,128)(2,1)S(1)} collective-permute-done((bf16[2,128,1536]{2,1,0:T(8,128)(2,1)S(1)}, bf16[2,128,1536]{2,1,0:T(8,128)(2,1)S(1)}, u32[]{:S(2)}, u32[]{:S(2)}) %collective-permute-start) | collective-permute-done | bytes 786464 | tf_op jit(solution)/shard_map/ppermute | solution.py:22
  23.0 0.0 copy-start.5
  23.0 0.0 copy-start.2
  23.0 0.0 copy-start.3
  23.0 2.4 %channelize.3 = (bf16[32,1,2,4,8,128]{5,4,3,2,1,0:T(8,128)(2,1)S(1)}, bf16[32,1,2,4,8,128]{5,4,3,2,1,0:T(8,128)(2,1)}) custom-call(bf16[2,128,2048]{2,1,0:T(8,128)(2,1)S(1)} %copy-done, bf16[2,128,1536]{2,1,0:T(8,128)(2,1)S(1)} %collective-permute-done.refs_1_, s32[4,512]{1,0:T(4,128)S(1)} %copy-done.4, f32[128,4]{1,0:T(8,128)S(1)} %reshape.35.refs_2_.refs_3_, ...), custom_call_target="tpu_custom_call" | custom-call | tf_op jit(solution)/shard_map/channelize/pallas_call | solution.py:116
  25.4 20.9 %all_to_all.10.refs_1_ = bf16[32,2,4,8,128]{4,3,2,1,0:T(8,128)(2,1)S(1)} all-to-all(bf16[32,2,4,8,128]{4,3,2,1,0:T(8,128)(2,1)S(1)} %bitcast.9), channel_id=1, replica_groups=mesh['inp'=8,'tim'=4] {'inp','tim'}, dimensions={0} | all-to-all | bytes 1048576 | tf_op jit(solution)/shard_map/all_to_all | solution.py:307
  46.3 4.1 %all-to-all-start = ((bf16[32,2,4,8,128]{4,3,2,1,0:T(8,128)(2,1)}), bf16[32,2,4,8,128]{4,3,2,1,0:T(8,128)(2,1)S(1)}, u32[]{:S(2)}, u32[]{:S(2)}) async-start(bf16[32,2,4,8,128]{4,3,2,1,0:T(8,128)(2,1)} %bitcast.1), calls=%async_computation | async-start | bytes 1048576 | tf_op jit(solution)/shard_map/all_to_all | solution.py:307
  50.4 0.0 copy-done.5
  50.4 0.3 select_reduce_fusion.refs_0_
  50.7 0.0 copy-done.2
  50.7 0.0 copy-done.3
  50.7 15.0 %correlate.2.refs_4_ = f32[16,528,16,128]{3,2,1,0:T(8,128)} custom-call(s32[1024]{0:T(1024)S(1)} %select_reduce_fusion.refs_0_, bf16[32,2,4,8,128]{4,3,2,1,0:T(8,128)(2,1)S(1)} %all_to_all.10.refs_1_, bf16[64,256]{1,0:T(8,128)(2,1)S(1)} %copy-done.3, bf16[128,512]{1,0:T(8,128)(2,1)S(1)} %copy-done.2), custom_call_target="tpu_custom_call" | custom-call | tf_op jit(solution)/shard_map/correlate/pallas_call | solution.py:257
  65.7 0.0 all-to-all-done.refs_1_
  65.7 14.9 %correlate.3 = f32[16,528,16,128]{3,2,1,0:T(8,128)} custom-call(s32[1024]{0:T(1024)S(1)} %select_reduce_fusion.refs_0_, bf16[32,2,4,8,128]{4,3,2,1,0:T(8,128)(2,1)S(1)} %all-to-all-done.refs_1_, bf16[64,256]{1,0:T(8,128)(2,1)S(1)} %copy-done.3, bf16[128,512]{1,0:T(8,128)(2,1)S(1)} %copy-done.2, ...), custom_call_target="tpu_custom_call", output_to_operand_aliasing={{}: (4, {})} | custom-call | tf_op jit(solution)/shard_map/correlate/pallas_call | solution.py:257
  (1 shorter events, 0.0 us)
Async XLA Ops:
  0.0 7.2 %copy-start = (bf16[2,128,2048]{2,1,0:T(8,128)(2,1)S(1)}, bf16[2,128,2048]{2,1,0:T(8,128)(2,1)}, u32[]{:S(2)}) copy-start(bf16[2,128,2048]{2,1,0:T(8,128)(2,1)} %refs_0_.3) | copy-start | bytes 3145732
  1.3 21.7 %collective-permute-start = (bf16[2,128,1536]{2,1,0:T(8,128)(2,1)S(1)}, bf16[2,128,1536]{2,1,0:T(8,128)(2,1)S(1)}, u32[]{:S(2)}, u32[]{:S(2)}) collective-permute-start(bf16[2,128,1536]{2,1,0:T(8,128)(2,1)S(1)} %slice.11), channel_id=1, source_target_pairs={{0,1},{1,2},{2,3},{4,5},{5,6},{6,7},{8,9},{9,10},{10,11},{12,13},{... | collective-permute-start | bytes 2359304 | tf_op jit(solution)/shard_map/ppermute | solution.py:22
  7.2 1.2 %copy-start.1 = (bf16[2,4,256,256]{3,2,1,0:T(8,128)(2,1)S(1)}, bf16[2,4,256,256]{3,2,1,0:T(8,128)(2,1)}, u32[]{:S(2)}) copy-start(bf16[2,4,256,256]{3,2,1,0:T(8,128)(2,1)} %constant.10.clone.refs_3_.refs_4_) | copy-start | bytes 3145732
  8.5 0.7 copy-start.4
  23.0 27.4 %copy-start.5 = (s32[528,2]{0,1:T(2,128)S(1)}, s32[528,2]{0,1:T(2,128)}, u32[]{:S(2)}) copy-start(s32[528,2]{0,1:T(2,128)} %param.13) | copy-start | bytes 12676
  23.0 27.7 %copy-start.2 = (bf16[128,512]{1,0:T(8,128)(2,1)S(1)}, bf16[128,512]{1,0:T(8,128)(2,1)}, u32[]{:S(2)}) copy-start(bf16[128,512]{1,0:T(8,128)(2,1)} %constant.12.clone.refs_3_) | copy-start | bytes 393220
  23.0 27.7 %copy-start.3 = (bf16[64,256]{1,0:T(8,128)(2,1)S(1)}, bf16[64,256]{1,0:T(8,128)(2,1)}, u32[]{:S(2)}) copy-start(bf16[64,256]{1,0:T(8,128)(2,1)} %constant.11.clone.refs_2_) | copy-start | bytes 98308
  46.3 19.4 %all-to-all-start = ((bf16[32,2,4,8,128]{4,3,2,1,0:T(8,128)(2,1)}), bf16[32,2,4,8,128]{4,3,2,1,0:T(8,128)(2,1)S(1)}, u32[]{:S(2)}, u32[]{:S(2)}) async-start(bf16[32,2,4,8,128]{4,3,2,1,0:T(8,128)(2,1)} %bitcast.1), calls=%async_computation | async-start | bytes 1048576 | tf_op jit(solution)/shard_map/all_to_all | solution.py:307

commit v3 on v2

--- a/solution.py
+++ b/solution.py
@@ -128,7 +128,7 @@
             jax.ShapeDtypeStruct((devices // sharers, sharers, group, spectra, 2 * strip, width), jnp.bfloat16)
             for group in groups
         ],
-        compiler_params=pltpu.CompilerParams(vmem_limit_bytes=40 << 20),
+        compiler_params=pltpu.CompilerParams(vmem_limit_bytes=16 << 20),
         name="channelize",
     )(voltages, *halos, fir_taps, flags, jnp.asarray(table), *started)
 
@@ -152,12 +152,12 @@
     span = tiles * tall
     zero = jnp.zeros((), jnp.bfloat16)
     lane = lax.broadcasted_iota(jnp.int32, (depth, width), 1) % PACK
-    lane_wide = lax.broadcasted_iota(jnp.int32, (depth, wide), 1) // TB % PACK
-
-    def unpack(i):
+    lane_pair = lax.broadcasted_iota(jnp.int32, (depth, 2 * LANES), 1) // TB % PACK
+
+    def unpack(i, residues_now):
         for t in range(n_times):
             for x_ref, first in zip(x_refs, firsts):
-                for q in range(group):
+                for q in residues_now:
                     for s in range(x_ref.shape[2]):
                         row = q * strip * depth + t * spectra + first + s
                         value = x_ref[i * n_times + t, q, s].astype(jnp.float32)
@@ -179,18 +179,16 @@
             preferred_element_type=jnp.float32,
         )
         left_ref[i * span : (i + 1) * span, :] = left.astype(jnp.bfloat16)
-        right = jnp.dot(plain, spread_ref[...], preferred_element_type=jnp.float32).astype(jnp.bfloat16)
-        for u in range(PACK):
-            right_ref[u * depth : (u + 1) * depth, i * wide : (i + 1) * wide] = jnp.where(
-                lane_wide == u, right, zero
-            )
+        right = jnp.dot(plain, spread_ref[...], preferred_element_type=jnp.float32)
+        right_ref[:, i * wide : (i + 1) * wide] = right.astype(jnp.bfloat16)
 
     def multiply(slot, pair):
         left_ref, right_ref, tile_ref = slots[slot]
         count = 2 * pair + 2
+        right = right_ref[:, pair * 2 * LANES : (pair + 1) * 2 * LANES]
         grid = jnp.dot(
             left_ref[0 : count * tall, :],
-            right_ref[:, pair * 2 * LANES : (pair + 1) * 2 * LANES],
+            jnp.concatenate([jnp.where(lane_pair == u, right, zero) for u in range(PACK)], axis=0),
             preferred_element_type=jnp.float32,
         )
         for first in range(count):
@@ -205,8 +203,9 @@
         target = channel % strip * residues + begin + channel // strip
         return pltpu.make_async_copy(slots[slot][2], out_ref.at[target], sems.at[slot])
 
+    now = 1 if strip > 1 else group
     for i in range(n_inputs):
-        unpack(i)
+        unpack(i, range(now))
         prepare(0, 0, i)
 
     def advance(index, carry):
@@ -225,10 +224,17 @@
                     prepare(channel, slot, i)
             for pair in range(pairs):
                 multiply(slot, pair)
-                if len(slots) > 1:
-                    for task in ahead[pair * n_inputs // pairs : (pair + 1) * n_inputs // pairs]:
-                        task()
             store(channel, slot).start()
+            if len(slots) > 1:
+                for task in ahead:
+                    task()
+            if slot == 0 and now < group:
+
+                @pl.when(index == 0)
+                def _():
+                    for i in range(n_inputs):
+                        unpack(i, range(now, group))
+
         return carry
 
     rounds = channels // len(slots)
@@ -272,13 +278,13 @@
         scratch_shapes=[pltpu.VMEM((n_inputs, channels * 2 * total, width), jnp.float32)]
         + [
             pltpu.VMEM((blocks * tall, deep), jnp.bfloat16),
-            pltpu.VMEM((deep, blocks * LANES), jnp.bfloat16),
+            pltpu.VMEM((2 * total, blocks * LANES), jnp.bfloat16),
             pltpu.VMEM((n_tiles, tall, LANES), jnp.float32),
         ]
         * slots
         + [pltpu.SemaphoreType.DMA((slots,))],
         input_output_aliases={3 + len(parts): 0} if earlier else {},
-        compiler_params=pltpu.CompilerParams(vmem_limit_bytes=48 << 20),
+        compiler_params=pltpu.CompilerParams(vmem_limit_bytes=24 << 20),
         name="correlate",
     )(place, *parts, jnp.asarray(pick, jnp.bfloat16), jnp.asarray(spread, jnp.bfloat16), *earlier)
 
@@ -301,6 +307,7 @@
     code = tile_pairs[:, 0] * blocks + tile_pairs[:, 1]
     match = jnp.arange(blocks * blocks, dtype=jnp.int32)[:, None] == code[None, :]
     place = jnp.sum(jnp.where(match, jnp.arange(n_tiles, dtype=jnp.int32)[None, :], 0), axis=1)
+    halo, place = lax.optimization_barrier((halo, place))
     own = taps - 1
     started = channelize(voltages, [], fir_taps, flags, own, spectra - own, groups, devices, [])
     spectra_groups = channelize(voltages, [halo], fir_taps, flags, 0, own, groups, devices, started)

time: 81 us -> 80.2 us (level)
  Pallas kernels: 33.1 us -> 31.9 us
    pallas_call x2, Pallas kernels: 29.9 us -> 28.7 us  [correlate(): pl.pallas_call(functools.partial(correlate_kernel, n_inputs=n_inputs, n_t...]
  transfers between devices with their start and end apart: 2 -> 2, of which waited for: 1 -> 1; matrix products, arithmetic and copies ran while one was open for 2% -> 2% of each run, Pallas kernels for 20% -> 19%
where the time goes in v3:
time: 80.2 us; the launch traced here: 79.1 us
  Pallas kernels  31.9 us (40%)
  blocking collectives  20.9 us (26%)
  waiting for transfers between devices  12.7 us (16%)
  starting transfers between devices  9.06 us (11%)
  local copies, waits for them, and re-layouts  3.5 us (4%)
  other arithmetic  0.97 us (1%)
    pallas_call x2, Pallas kernels, correlate(): pl.pallas_call(functools.partial(correlate_kernel, n_inputs=n_inputs, n_t...  28.7 us
    all_to_all x1, blocking collectives, body(): exchange(part.reshape((devices,) + part.shape[2:]))  20.9 us
    ppermute x1, waiting for transfers between devices, shifted(): return lax.ppermute(block, axis, route)  12.7 us
    ppermute x1, starting transfers between devices, shifted(): return lax.ppermute(block, axis, route)  4.98 us
    all_to_all x1, starting transfers between devices, body(): exchange(part.reshape((devices,) + part.shape[2:]))  4.08 us
    pallas_call x2, Pallas kernels, channelize(): pl.pallas_call(functools.partial(channelize_kernel, taps=taps, chans=chan...  3.16 us
    unnamed x12, local copies, waits for them, and re-layouts  1.94 us
  transfers between devices with their start and end apart: 2, of which 1 were waited for; matrix products, arithmetic and copies ran while one was open for 2% of the time, Pallas kernels for 19%

profile of v3, /device:TPU:0, one launch (start us, length us, event | category | flops | bytes accessed | tf_op | source)
XLA Modules:
  0.0 79.1 jit_solution(156513346056906717)
XLA Ops:
  0.0 0.0 copy-start
  0.0 0.0 copy-start.5
  0.0 1.3 %slice.9 = bf16[2,128,1536]{2,1,0:T(8,128)(2,1)S(1)} slice(bf16[2,128,2048]{2,1,0:T(8,128)(2,1)} %refs_0_.3), slice={[0:2], [0:128], [512:2048]} | slice | bytes 1572864 | tf_op jit(solution)/shard_map/slice | solution.py:301
  1.3 5.0 %collective-permute-start = (bf16[2,128,1536]{2,1,0:T(8,128)(2,1)S(1)}, bf16[2,128,1536]{2,1,0:T(8,128)(2,1)S(1)}, u32[]{:S(2)}, u32[]{:S(2)}) collective-permute-start(bf16[2,128,1536]{2,1,0:T(8,128)(2,1)S(1)} %slice.9), channel_id=1, source_target_pairs={{0,1},{1,2},{2,3},{4,5},{5,6},{6,7},{8,9},{9,10},{10,11},{12,13},{... | collective-permute-start | bytes 2359304 | tf_op jit(solution)/shard_map/ppermute | solution.py:22
  6.3 0.7 convert_bitcast_fusion
  6.9 0.1 broadcast_in_dim.21
  7.0 0.1 convert_element_type.9
  7.1 0.1 reshape.35.refs_2_.refs_3_
  7.2 0.0 copy-done
  7.2 0.0 copy-start.1
  7.2 1.2 %copy-done.1 = bf16[2,4,256,256]{3,2,1,0:T(8,128)(2,1)S(1)} copy-done((bf16[2,4,256,256]{3,2,1,0:T(8,128)(2,1)S(1)}, bf16[2,4,256,256]{3,2,1,0:T(8,128)(2,1)}, u32[]{:S(2)}) %copy-start.1) | copy-done | bytes 1048600
  8.5 0.0 copy-start.4
  8.5 0.7 copy-done.4
  9.2 0.8 %channelize.2 = (bf16[32,1,2,1,8,128]{5,4,3,2,1,0:T(8,128)(2,1)S(1)}, bf16[32,1,2,1,8,128]{5,4,3,2,1,0:T(8,128)(2,1)S(1)}) custom-call(bf16[2,128,2048]{2,1,0:T(8,128)(2,1)S(1)} %copy-done, s32[4,512]{1,0:T(4,128)S(1)} %copy-done.4, f32[128,4]{1,0:T(8,128)S(1)} %reshape.35.refs_2_.refs_3_, bf16[2,4,256,256]{3,2,1,0:T(8,128)(2,1)S(1)} %copy-done.1), custom_call_target="tpu_custom_call" | custom-call | tf_op jit(solution)/shard_map/channelize/pallas_call | solution.py:116
  10.0 0.0 copy-done.5
  10.0 0.3 select_reduce_fusion.refs_0_
  10.3 12.7 %collective-permute-done.refs_1_ = bf16[2,128,1536]{2,1,0:T(8,128)(2,1)S(1)} collective-permute-done((bf16[2,128,1536]{2,1,0:T(8,128)(2,1)S(1)}, bf16[2,128,1536]{2,1,0:T(8,128)(2,1)S(1)}, u32[]{:S(2)}, u32[]{:S(2)}) %collective-permute-start) | collective-permute-done | bytes 786464 | tf_op jit(solution)/shard_map/ppermute | solution.py:22
  23.0 0.0 copy-start.2
  23.0 0.0 copy-start.3
  23.0 2.4 %channelize.3 = (bf16[32,1,2,4,8,128]{5,4,3,2,1,0:T(8,128)(2,1)S(1)}, bf16[32,1,2,4,8,128]{5,4,3,2,1,0:T(8,128)(2,1)}) custom-call(bf16[2,128,2048]{2,1,0:T(8,128)(2,1)S(1)} %copy-done, bf16[2,128,1536]{2,1,0:T(8,128)(2,1)S(1)} %collective-permute-done.refs_1_, s32[4,512]{1,0:T(4,128)S(1)} %copy-done.4, f32[128,4]{1,0:T(8,128)S(1)} %reshape.35.refs_2_.refs_3_, ...), custom_call_target="tpu_custom_call" | custom-call | tf_op jit(solution)/shard_map/channelize/pallas_call | solution.py:116
  25.4 20.9 %all_to_all.10.refs_1_ = bf16[32,2,4,8,128]{4,3,2,1,0:T(8,128)(2,1)S(1)} all-to-all(bf16[32,2,4,8,128]{4,3,2,1,0:T(8,128)(2,1)S(1)} %bitcast.9), channel_id=1, replica_groups=mesh['inp'=8,'tim'=4] {'inp','tim'}, dimensions={0} | all-to-all | bytes 1048576 | tf_op jit(solution)/shard_map/all_to_all | solution.py:314
  46.3 4.1 %all-to-all-start = ((bf16[32,2,4,8,128]{4,3,2,1,0:T(8,128)(2,1)}), bf16[32,2,4,8,128]{4,3,2,1,0:T(8,128)(2,1)S(1)}, u32[]{:S(2)}, u32[]{:S(2)}) async-start(bf16[32,2,4,8,128]{4,3,2,1,0:T(8,128)(2,1)} %bitcast.1), calls=%async_computation | async-start | bytes 1048576 | tf_op jit(solution)/shard_map/all_to_all | solution.py:314
  50.4 0.0 copy-done.2
  50.4 0.0 copy-done.3
  50.4 14.3 %correlate.2.refs_4_ = f32[16,528,16,128]{3,2,1,0:T(8,128)} custom-call(s32[1024]{0:T(1024)S(1)} %select_reduce_fusion.refs_0_, bf16[32,2,4,8,128]{4,3,2,1,0:T(8,128)(2,1)S(1)} %all_to_all.10.refs_1_, bf16[64,256]{1,0:T(8,128)(2,1)S(1)} %copy-done.3, bf16[128,512]{1,0:T(8,128)(2,1)S(1)} %copy-done.2), custom_call_target="tpu_custom_call" | custom-call | tf_op jit(solution)/shard_map/correlate/pallas_call | solution.py:263
  64.7 0.0 all-to-all-done.refs_1_
  64.8 14.4 %correlate.3 = f32[16,528,16,128]{3,2,1,0:T(8,128)} custom-call(s32[1024]{0:T(1024)S(1)} %select_reduce_fusion.refs_0_, bf16[32,2,4,8,128]{4,3,2,1,0:T(8,128)(2,1)S(1)} %all-to-all-done.refs_1_, bf16[64,256]{1,0:T(8,128)(2,1)S(1)} %copy-done.3, bf16[128,512]{1,0:T(8,128)(2,1)S(1)} %copy-done.2, ...), custom_call_target="tpu_custom_call", output_to_operand_aliasing={{}: (4, {})} | custom-call | tf_op jit(solution)/shard_map/correlate/pallas_call | solution.py:263
  (1 shorter events, 0.0 us)
Async XLA Ops:
  0.0 7.2 %copy-start = (bf16[2,128,2048]{2,1,0:T(8,128)(2,1)S(1)}, bf16[2,128,2048]{2,1,0:T(8,128)(2,1)}, u32[]{:S(2)}) copy-start(bf16[2,128,2048]{2,1,0:T(8,128)(2,1)} %refs_0_.3) | copy-start | bytes 3145732
  0.0 10.0 %copy-start.5 = (s32[528,2]{0,1:T(2,128)S(1)}, s32[528,2]{0,1:T(2,128)}, u32[]{:S(2)}) copy-start(s32[528,2]{0,1:T(2,128)} %param.13) | copy-start | bytes 12676
  1.3 21.7 %collective-permute-start = (bf16[2,128,1536]{2,1,0:T(8,128)(2,1)S(1)}, bf16[2,128,1536]{2,1,0:T(8,128)(2,1)S(1)}, u32[]{:S(2)}, u32[]{:S(2)}) collective-permute-start(bf16[2,128,1536]{2,1,0:T(8,128)(2,1)S(1)} %slice.9), channel_id=1, source_target_pairs={{0,1},{1,2},{2,3},{4,5},{5,6},{6,7},{8,9},{9,10},{10,11},{12,13},{... | collective-permute-start | bytes 2359304 | tf_op jit(solution)/shard_map/ppermute | solution.py:22
  7.2 1.2 %copy-start.1 = (bf16[2,4,256,256]{3,2,1,0:T(8,128)(2,1)S(1)}, bf16[2,4,256,256]{3,2,1,0:T(8,128)(2,1)}, u32[]{:S(2)}) copy-start(bf16[2,4,256,256]{3,2,1,0:T(8,128)(2,1)} %constant.10.clone.refs_3_.refs_4_) | copy-start | bytes 3145732
  8.5 0.7 copy-start.4
  23.0 27.4 %copy-start.2 = (bf16[128,512]{1,0:T(8,128)(2,1)S(1)}, bf16[128,512]{1,0:T(8,128)(2,1)}, u32[]{:S(2)}) copy-start(bf16[128,512]{1,0:T(8,128)(2,1)} %constant.12.clone.refs_3_) | copy-start | bytes 393220
  23.0 27.4 %copy-start.3 = (bf16[64,256]{1,0:T(8,128)(2,1)S(1)}, bf16[64,256]{1,0:T(8,128)(2,1)}, u32[]{:S(2)}) copy-start(bf16[64,256]{1,0:T(8,128)(2,1)} %constant.11.clone.refs_2_) | copy-start | bytes 98308
  46.3 18.5 %all-to-all-start = ((bf16[32,2,4,8,128]{4,3,2,1,0:T(8,128)(2,1)}), bf16[32,2,4,8,128]{4,3,2,1,0:T(8,128)(2,1)S(1)}, u32[]{:S(2)}, u32[]{:S(2)}) async-start(bf16[32,2,4,8,128]{4,3,2,1,0:T(8,128)(2,1)} %bitcast.1), calls=%async_computation | async-start | bytes 1048576 | tf_op jit(solution)/shard_map/all_to_all | solution.py:314
